TPU v7x, 32 devices: a whole 2x2x4 slice. The times are simulated.
32 devices in a mesh: dp: 8 (over z, y), tensor: 4 (over x, core).
Axes of the slice: x: 2, y: 2, z: 4, core: 2. Of those that a mesh axis runs over, the one named last changes fastest.
Arguments:
- hidden: bfloat16 [12288, 1536], P('dp'), may hold values from -6 to 6
- segment_ids: int32 [12288], P('dp'), may hold values from -1 to 12287, as said below
- norm_gain: float32 [1536], replicated, may hold values from 0.5 to 1.5
- gate_weight: bfloat16 [1536, 3072], P(None, 'tensor'), may hold values from -0.15625 to 0.15625
- input_weight: bfloat16 [1536, 3072], P(None, 'tensor'), may hold values from -0.15625 to 0.15625
- step_weight: bfloat16 [1536, 48], P(None, 'tensor'), may hold values from -0.15625 to 0.15625
- state_weight: bfloat16 [1536, 256], replicated, may hold values from -0.15625 to 0.15625
- conv_weight: float32 [4, 3072], P(None, 'tensor'), may hold values from -3 to 3
- state_conv_weight: float32 [4, 256], replicated, may hold values from -3 to 3
- conv_bias: float32 [3072], P('tensor'), may hold values from -0.5 to 0.5
- state_conv_bias: float32 [256], replicated, may hold values from -0.5 to 0.5
- step_bias: float32 [48], P('tensor'), may hold values from -6.9 to -2.25
- decay_log: float32 [48], P('tensor'), may hold values from 0 to 2.77
- skip_gain: float32 [48], P('tensor'), may hold values from 0.5 to 1.5
- gate_norm_gain: float32 [3072], P('tensor'), may hold values from 0.5 to 1.5
- out_weight: bfloat16 [3072, 1536], P('tensor'), may hold values from -0.109375 to 0.109375
- cotangent: bfloat16 [12288, 1536], P('dp'), may hold values from -6 to 6
Outputs:
- block_out: bfloat16 [12288, 1536], P('dp')
- grad_hidden: float32 [12288, 1536], P('dp')
- grad_norm_gain: float32 [1536], replicated
- grad_gate_weight: float32 [1536, 3072], P(None, 'tensor')
- grad_input_weight: float32 [1536, 3072], P(None, 'tensor')
- grad_step_weight: float32 [1536, 48], P(None, 'tensor')
- grad_state_weight: float32 [1536, 256], replicated
- grad_conv_weight: float32 [4, 3072], P(None, 'tensor')
- grad_state_conv_weight: float32 [4, 256], replicated
- grad_conv_bias: float32 [3072], P('tensor')
- grad_state_conv_bias: float32 [256], replicated
- grad_step_bias: float32 [48], P('tensor')
- grad_decay_log: float32 [48], P('tensor')
- grad_skip_gain: float32 [48], P('tensor')
- grad_gate_norm_gain: float32 [3072], P('tensor')
- grad_out_weight: float32 [3072, 1536], P('tensor')
Inputs may be any that keep to these rules, and one draw needn't show every extreme that they name: `segment_ids`: each value is -1 for an empty slot or the global index of the first slot of its sequence; a sequence lies within the 1536 slots of one dp index, its slots are consecutive; the empty slots of a dp index come after all its sequences and number a multiple of 256; the last dp index has no empty slot, and the last slot of all starts a sequence of one token.
All inputs are finite; a program needn't handle non-finite values.
Results may differ from a plain program's by a relative error of at most 0.0096.
Values may be sent and summed in bfloat16 or wider, within the bound.
No kernel may reach another device: no remote copies, remote signals or barrier semaphores. Data moves between devices by JAX's collectives and lax.ppermute only.
A program may use at most 256 MiB of HBM per device.

v0:
```python
from functools import partial
import jax
import jax.numpy as jnp
from jax import lax
from jax.sharding import PartitionSpec as P

INNER = 3072
GROUP = 256
EPS = 1e-05
HIGH = lax.Precision.HIGHEST


def conv_silu(inputs, weights, biases, segments):
    summed = biases[None, :] + weights[0][None, :] * inputs
    for offset in range(1, weights.shape[0]):
        shifted = jnp.concatenate(
            [jnp.zeros((offset, inputs.shape[1]), inputs.dtype), inputs[:-offset]], axis=0
        )
        seg_shift = jnp.concatenate([jnp.full((offset,), -2, jnp.int32), segments[:-offset]])
        keeping = (seg_shift == segments).astype(inputs.dtype)
        summed = summed + weights[offset][None, :] * shifted * keeping[:, None]
    return jax.nn.silu(summed)


def ssd_scan(values, states, step_raw, step_bias, decay_log, skip_gain, segments, group):
    length = values.shape[0]
    heads = step_bias.shape[0]
    width = values.shape[1] // heads
    state = states.shape[1] // 2
    blocks = length // group
    step = jax.nn.softplus(step_raw + step_bias[None, :])
    rate = step * (-jnp.exp(decay_log))[None, :]
    x_blk = values.reshape(blocks, group, heads, width)
    b_blk = states[:, :state].reshape(blocks, group, state)
    c_blk = states[:, state:].reshape(blocks, group, state)
    step_h = step.reshape(blocks, group, heads).transpose(0, 2, 1)
    cum_h = jnp.cumsum(rate.reshape(blocks, group, heads), axis=1).transpose(0, 2, 1)
    seg_blk = segments.reshape(blocks, group)
    causal = jnp.tril(jnp.ones((group, group), bool))
    same = ((seg_blk[:, :, None] == seg_blk[:, None, :]) & causal[None])[:, None]
    differ = cum_h[:, :, :, None] - cum_h[:, :, None, :]
    decay = jnp.where(same, jnp.exp(jnp.where(same, differ, 0.0)), 0.0)
    inner_cb = jnp.einsum("cin,cjn->cij", c_blk, b_blk, precision=HIGH)
    mixing = decay * inner_cb[:, None] * step_h[:, :, None, :]
    y_diag = jnp.einsum("chij,cjhp->cihp", mixing, x_blk, precision=HIGH)
    last_seg = seg_blk[:, -1]
    to_end = jnp.exp(cum_h[:, :, -1:] - cum_h) * step_h * (seg_blk == last_seg[:, None])[:, None, :]
    weighted = to_end.transpose(0, 2, 1)[..., None] * x_blk
    local_state = jnp.einsum("cjn,cjhp->chnp", b_blk, weighted, precision=HIGH)
    prev_seg = jnp.concatenate([jnp.full((1,), -3, jnp.int32), last_seg[:-1]])
    carry_keep = (last_seg == prev_seg).astype(values.dtype)[:, None] * jnp.exp(cum_h[:, :, -1])

    def advance(entering, pieces):
        local_part, factor = pieces
        return (local_part + factor[:, None, None] * entering, entering)

    start_state = jnp.zeros((heads, state, width), values.dtype)
    _, entering_all = lax.scan(advance, start_state, (local_state, carry_keep))
    reach = jnp.exp(cum_h).transpose(0, 2, 1) * (seg_blk == prev_seg[:, None])[..., None]
    y_off = jnp.einsum("cin,chnp->cihp", c_blk, entering_all, precision=HIGH) * reach[..., None]
    result = y_diag + y_off + skip_gain[None, None, :, None] * x_blk
    return result.reshape(length, heads * width)


def cross_dot(left, right):
    return lax.dot_general(
        left, right, (((0,), (0,)), ((), ())), preferred_element_type=jnp.float32
    )


def back_dot(left, right):
    return lax.dot_general(
        left, right, (((1,), (1,)), ((), ())), preferred_element_type=jnp.float32
    )


def body(
    hidden,
    segment_ids,
    norm_gain,
    gate_weight,
    input_weight,
    step_weight,
    state_weight,
    conv_weight,
    state_conv_weight,
    conv_bias,
    state_conv_bias,
    step_bias,
    decay_log,
    skip_gain,
    gate_norm_gain,
    out_weight,
    cotangent,
):
    valid = (segment_ids >= 0).astype(jnp.float32)[:, None]
    hidden_f = hidden.astype(jnp.float32)
    inverse = lax.rsqrt(jnp.mean(hidden_f * hidden_f, axis=1, keepdims=True) + EPS)
    normed = (hidden_f * inverse * norm_gain[None, :]).astype(jnp.bfloat16)
    gate_pre = jnp.dot(normed, gate_weight, preferred_element_type=jnp.float32)
    input_pre = jnp.dot(normed, input_weight, preferred_element_type=jnp.float32)
    step_pre = jnp.dot(normed, step_weight, preferred_element_type=jnp.float32)
    state_pre = jnp.dot(normed, state_weight, preferred_element_type=jnp.float32)
    conv_out, conv_back = jax.vjp(
        partial(conv_silu, segments=segment_ids), input_pre, conv_weight, conv_bias
    )
    state_out, state_back = jax.vjp(
        partial(conv_silu, segments=segment_ids), state_pre, state_conv_weight, state_conv_bias
    )
    values_f = lax.optimization_barrier(conv_out.astype(jnp.bfloat16)).astype(jnp.float32)
    states_f = lax.optimization_barrier(state_out.astype(jnp.bfloat16)).astype(jnp.float32)
    mixed_y, ssd_back = jax.vjp(
        partial(ssd_scan, segments=segment_ids, group=GROUP),
        values_f,
        states_f,
        step_pre,
        step_bias,
        decay_log,
        skip_gain,
    )
    gate_act = jax.nn.silu(gate_pre)
    gated = mixed_y * gate_act
    square_sum = lax.psum(jnp.sum(gated * gated, axis=1), "tensor")
    gate_inverse = lax.rsqrt(square_sum / INNER + EPS)[:, None]
    gnormed = (gated * gate_inverse * gate_norm_gain[None, :]).astype(jnp.bfloat16)
    partial_mix = jnp.dot(gnormed, out_weight, preferred_element_type=jnp.float32)
    mix = lax.psum(partial_mix, "tensor")
    block_out = (hidden_f + valid * mix).astype(jnp.bfloat16)
    dmix = (cotangent.astype(jnp.float32) * valid).astype(jnp.bfloat16)
    grad_out = cross_dot(gnormed, dmix)
    d_gn = back_dot(dmix, out_weight)
    grad_gnorm = jnp.sum(d_gn * gated * gate_inverse, axis=0)
    scaled = d_gn * gate_norm_gain[None, :]
    dot_sum = lax.psum(jnp.sum(gated * scaled, axis=1), "tensor")
    d_gated = gate_inverse * scaled - gated * gate_inverse**3 * (dot_sum / INNER)[:, None]
    d_y = d_gated * gate_act
    sigma = jax.nn.sigmoid(gate_pre)
    d_gate = d_gated * mixed_y * sigma * (1.0 + gate_pre * (1.0 - sigma))
    d_values, d_states, d_step, grad_sbias, grad_decay, grad_skip = ssd_back(d_y)
    d_input, grad_conv, grad_cbias = conv_back(d_values)
    gate_b = d_gate.astype(jnp.bfloat16)
    input_b = d_input.astype(jnp.bfloat16)
    step_b = d_step.astype(jnp.bfloat16)
    local_back = (
        back_dot(gate_b, gate_weight)
        + back_dot(input_b, input_weight)
        + back_dot(step_b, step_weight)
    )
    summed_back, states_full = lax.psum((local_back, d_states), "tensor")
    d_state_pre, grad_sconv, grad_scbias = state_back(states_full)
    state_b = d_state_pre.astype(jnp.bfloat16)
    d_normed = summed_back + back_dot(state_b, state_weight)
    grad_norm = jnp.sum(d_normed * hidden_f * inverse, axis=0)
    scaled_in = d_normed * norm_gain[None, :]
    grad_hidden = (
        cotangent.astype(jnp.float32)
        + inverse * scaled_in
        - hidden_f * inverse**3 * jnp.mean(hidden_f * scaled_in, axis=1, keepdims=True)
    )
    grad_gate = cross_dot(normed, gate_b)
    grad_input = cross_dot(normed, input_b)
    grad_step = cross_dot(normed, step_b)
    grad_state = cross_dot(normed, state_b)
    summed = lax.psum(
        (
            grad_norm,
            grad_gate,
            grad_input,
            grad_step,
            grad_state,
            grad_conv,
            grad_sconv,
            grad_cbias,
            grad_scbias,
            grad_sbias,
            grad_decay,
            grad_skip,
            grad_gnorm,
            grad_out,
        ),
        "dp",
    )
    (
        grad_norm,
        grad_gate,
        grad_input,
        grad_step,
        grad_state,
        grad_conv,
        grad_sconv,
        grad_cbias,
        grad_scbias,
        grad_sbias,
        grad_decay,
        grad_skip,
        grad_gnorm,
        grad_out,
    ) = summed
    return (
        block_out,
        grad_hidden,
        grad_norm,
        grad_gate,
        grad_input,
        grad_step,
        grad_state,
        grad_conv,
        grad_sconv,
        grad_cbias,
        grad_scbias,
        grad_sbias,
        grad_decay,
        grad_skip,
        grad_gnorm,
        grad_out,
    )


def solution(mesh):
    return jax.shard_map(
        body,
        mesh=mesh,
        in_specs=(
            P("dp", None),
            P("dp"),
            P(),
            P(None, "tensor"),
            P(None, "tensor"),
            P(None, "tensor"),
            P(),
            P(None, "tensor"),
            P(),
            P("tensor"),
            P(),
            P("tensor"),
            P("tensor"),
            P("tensor"),
            P("tensor"),
            P("tensor", None),
            P("dp", None),
        ),
        out_specs=(
            P("dp", None),
            P("dp", None),
            P(),
            P(None, "tensor"),
            P(None, "tensor"),
            P(None, "tensor"),
            P(),
            P(None, "tensor"),
            P(),
            P("tensor"),
            P(),
            P("tensor"),
            P("tensor"),
            P("tensor"),
            P("tensor"),
            P("tensor", None),
        ),
        check_vma=False,
    )
```

profile of v0, /device:TPU:0, one launch (start us, length us, event | category | flops | bytes accessed | tf_op | source)
XLA Modules:
  0.0 1345.6 jit_solution(4326663023551138808)
XLA Ops:
  14.4 4.0 fusion.117
  19.1 6.8 multiply_convert_fusion.2
  25.9 8.5 reshape.327
  34.3 8.2 reshape.326
  43.2 4.3 compare_select_fusion.2
  51.8 9.9 copy.178
  61.7 3.8 fusion.118
  71.5 3.8 fusion.67
  78.2 42.7 %while.34 = (s32[]{:T(128)}, f32[12,128,64]{2,1,0:T(8,128)}, f32[6,12,128,64]{3,2,1,0:T(8,128)}, f32[6,12,1,1]{1,3,2,0:T(1,128)}, f32[6,12,128,64]{2,3,1,0:T(8,128)}, /*index=5*/f32[6,12]{1,0:T(8,128)}, s32[]{:T(128)}, s32[]{:T(128)}) while((s32[]{:T(128)}, f32[12,128,64]{2,1,0:T(8,128)}, f32[6,12,128,64]{3,2,1,0:T(8,128)}, ...), condition=%wide.region_4.5_spmd.clone, body=%wide.region_3.4_spmd.clone.sunk | while | flops 393219 | bytes 4327672 | solution.py:58
  120.9 5.4 copy.180
  126.3 5.9 fusion.120
  133.8 7.4 copy.176
  142.3 18.5 %fusion.40 = f32[6,256,12,64]{1,3,2,0:T(8,128)} fusion(f32[6,256,12,64]{1,3,2,0:T(8,128)} %copy.178, f32[6,256,12,64]{1,3,2,0:T(8,128)} %bitcast.225, f32[12]{0:T(128)S(1)} %copy-done.91, f32[6,256,12]{1,2,0:T(8,128)S(1)} %copy-done.30, bf16[6,256,12,64]{1,3,2,0:T(8,128)(2,1)} %copy.176, f32[6,12,256]{2,1,0:T(8,128)S(1)} %bitcast.258, ...), kind=kOutput, calls=%fused_computation.68 | convolution fusion | flops 3652190208 | bytes 18702384 | tf_op jit(solution)/shard_map/jvp(chij,cjhp->cihp)/dot_general | solution.py:45
  160.7 10.7 copy.219
  171.5 9.9 reshape.328
  181.4 10.2 multiply_reduce_fusion.11
  191.7 8.5 psum.133
  200.2 11.6 multiply_reduce_fusion.2
  211.8 6.0 psum.135
  217.9 12.3 multiply_reduce_fusion.3
  230.1 6.1 copy.185
  236.2 6.9 reshape.302
  243.1 19.8 %fusion.77 = f32[6,256,128]{2,1,0:T(8,128)} fusion(f32[6,12,128,64]{3,2,1,0:T(8,128)} %get-tuple-element.547, f32[6,256,12]{1,2,0:T(8,128)S(1)} %copy-done.30, f32[6,256,12,64]{1,0,3,2:T(8,128)} %reshape.302), kind=kOutput, calls=%fused_computation.129 | convolution fusion | flops 1813118976 | bytes 7938048 | tf_op jit(solution)/shard_map/transpose(jvp(cin,chnp->cihp))/dot_general | solution.py:60
  262.9 5.1 multiply_reduce_fusion.8
  268.0 4.9 fusion.70
  276.3 45.5 %while.35 = (s32[]{:T(128)}, f32[12,128,64]{2,1,0:T(8,128)}, f32[6,12,128,64]{3,2,1,0:T(8,128)}, f32[6,12]{1,0:T(8,128)}, f32[6,12,128,64]{2,3,1,0:T(8,128)}, /*...) while((s32[]{:T(128)}, f32[12,128,64]{2,1,0:T(8,128)}, ...), condition=%wide.region_12.13_spmd.clone, body=%wide.region_10.12_spmd.clone.sunk | while | flops 589816 | bytes 4719024 | solution.py:58
  321.8 18.7 %fusion.80 = f32[6,256,128]{2,1,0:T(8,128)S(1)} fusion(f32[6,12,128,64]{3,2,1,0:T(8,128)} %get-tuple-element.193, f32[6,256,12,64]{1,3,2,0:T(8,128)} %copy.178, f32[6,256,12]{1,2,0:T(8,128)} %copy-done.28), kind=kOutput, calls=%fused_computation.130 | convolution fusion | flops 1813118976 | bytes 7938048 | tf_op jit(solution)/shard_map/transpose(jvp(cjn,cjhp->chnp))/dot_general | solution.py:49
  340.6 8.7 multiply_reduce_fusion.9
  349.4 6.8 fusion.106
  356.2 23.7 %fusion.11 = (f32[6,12,256]{2,1,0:T(8,128)}, f32[6,12,256]{2,1,0:T(8,128)}, f32[6,12,256]{2,1,0:T(8,128)}, f32[6,256,256]{2,1,0:T(8,128)S(1)}) fusion(f32[6,12,256]{2,1,0:T(8,128)S(1)} %bitcast.259, f32[6,256,256]{2,1,0:T(8,128)S(1)} %copy-done.26, f32[6,12,256]{2,1,0:T(8,128)S(1)} %copy-done.25, pred[6,256,256]{2,1,0:T(8,128)(4,1)S(1)} %copy-done.35, ...), kind=kOutput, calls=%fused_computation.31 | convolution fusion | flops 3694209024 | bytes 10985472 | tf_op jit(solution)/shard_map/transpose(jvp(chij,cjhp->cihp))/dot_general | solution.py:45
  386.4 14.9 %reduce-window.16 = f32[6,12,2,128]{3,1,2,0:T(8,128)S(1)} reduce-window(f32[6,12,2,128]{3,1,2,0:T(8,128)S(1)} %copy.201, f32[]{:T(128)} %constant.111.clone.1), window={size=1x1x1x128 pad=0_0x0_0x0_0x0_127}, to_apply=%region_19.20 | reduce-window | flops 2340864 | bytes 147460 | tf_op jit(solution)/shard_map/reduce-window.2
  401.9 24.5 %bitcast_add_fusion.2 = f32[6,256,12,64]{1,3,2,0:T(8,128)} fusion(f32[6,256,12,64]{1,3,2,0:T(8,128)} %get-tuple-element.428, f32[12]{0:T(128)} %param.34, f32[6,256,12]{1,2,0:T(8,128)S(1)} %copy-done.29, f32[6,12,256]{2,1,0:T(8,128)} %bitcast.257, f32[6,256,256]{2,1,0:T(8,128)} %fusion.119, f32[6,12,256]{2,1,0:T(8,128)S(1)} %copy-done.25, ...), kind=kOutput, calls=%fused_computation.62 | convolution fusion | flops 3652190208 | bytes 21061680 | tf_op jit(solution)/shard_map/transpose(jvp(chij,cjhp->cihp))/dot_general | solution.py:45
  426.4 10.7 copy.221
  437.2 10.0 reshape.329
  447.2 9.5 multiply_reduce_fusion.7
  465.4 6.5 fusion.122
  472.0 4.0 fusion.121
  477.5 5.1 convolution_add_fusion.1
  482.9 3.9 fusion.97
  486.8 9.4 fusion.124
  496.2 8.7 fusion.123
  504.9 6.7 fusion.63
  511.6 318.8 %all-reduce.34.cloned.1.call-done = (f32[1536,1536]{1,0:T(8,128)}, f32[1536,1536]{1,0:T(8,128)}, f32[1536,256]{1,0:T(8,128)}) async-done(((f32[1536,1536]{1,0:T(8,128)}, f32[1536,1536]{1,0:T(8,128)}, f32[1536,256]{1,0:T(8,128)}), (f32[1536,1536]{1,0:T(8,128)}, f32[1536,1536]{1,0:T(8,128)}, f32[1536,256]{1,0:T(8,128)})) %all-reduce.34.cloned.1.call-update) | async-done | bytes 20447248 | tf_op jit(solution)/shard_map/psum | solution.py:127
  841.0 9.4 fusion.21
  850.4 40.7 %all-reduce.26 = (f32[1536]{0:T(1024)}, f32[4,768]{1,0:T(4,128)}, f32[4,256]{1,0:T(4,128)}, f32[768]{0:T(1024)}, f32[256]{0:T(256)}, /*index=5*/f32[12]{0:T(128)}, f32[12]{0:T(128)}, f32[12]{0:T(128)}, f32[768]{0:T(1024)}) all-reduce(f32[1536]{0:T(1024)S(1)} %get-tuple-element.309, ...), channel_id=1, replica_groups=mesh['dp'=8,'tensor'=4] {'dp'}, use_global_device_ids=true, to_apply=%region_26.27 | all-reduce | flops 7460 | bytes 59680 | tf_op jit(solution)/shard_map/psum | solution.py:164
  891.1 17.0 %fusion.13 = (f32[1536,1536]{1,0:T(8,128)}, bf16[1536,1536]{1,0:T(8,128)(2,1)}) fusion(bf16[1536,1536]{1,0:T(8,128)(2,1)} %param.37, bf16[1536,1536]{1,0:T(8,128)(2,1)} %param.21, f32[1536,1536]{1,0:T(8,128)} %get-tuple-element.429, f32[1536]{0:T(1024)S(1)} %broadcast_multiply_fusion.8, f32[1536]{0:T(1024)S(1)} %copy-done.68, f32[1536]{0:T(1024)S(1)} %copy-done.55, ...), kind=kLoop, calls=%fused_computation.35 | loop fusion | flops 25952256 | bytes 42498048 | tf_op jit(solution)/shard_map/sub | solution.py:156
  908.1 418.2 %all-reduce.32.cloned.1.call-done = (f32[1536,768]{1,0:T(8,128)}, f32[1536,768]{1,0:T(8,128)}, f32[1536,12]{0,1:T(8,128)}, f32[1536,256]{1,0:T(8,128)}, f32[768,1536]{1,0:T(8,128)}) async-done(((f32[1536,768]{1,0:T(8,128)}, f32[1536,768]{1,0:T(8,128)}, f32[1536,12]{0,1:T(8,128)}, f32[1536,256]{1,0:T(8,128)}, f32[768,1536]{1,0:T(8,128)}), (f32[1536,768]{1,0:T(8,128)}, f32[1536,768]{1,0:T(8,128)}, ...) | async-done | bytes 15802384 | tf_op jit(solution)/shard_map/psum | solution.py:164
  1326.3 5.2 copy.308
  (400 shorter events, 150.2 us)
Async XLA Ops:
  7.2 174.3 %copy-start = (bf16[1536,768]{1,0:T(8,128)(2,1)S(1)}, bf16[1536,768]{1,0:T(8,128)(2,1)}, u32[]{:S(2)}) copy-start(bf16[1536,768]{1,0:T(8,128)(2,1)} %param.24) | copy-start | bytes 7077892
  7.2 823.2 %all-reduce.34.cloned.1.call-start = ((), (), s32[]{:S(2)}) async-start(), calls=%async_computation.1 | async-start | bytes 40894464 | tf_op jit(solution)/shard_map/psum | solution.py:127
  18.4 7.5 copy-start.1
  19.1 46.5 %copy-start.37 = (f32[1536]{0:T(1024)}, f32[1536]{0:T(1024)S(1)}, u32[]{:S(2)}) copy-start(f32[1536]{0:T(1024)S(1)} %get-tuple-element.415) | copy-start | bytes 18436
  19.1 46.5 %copy-start.39 = (f32[1536]{0:T(1024)}, f32[1536]{0:T(1024)S(1)}, u32[]{:S(2)}) copy-start(f32[1536]{0:T(1024)S(1)} %get-tuple-element.413) | copy-start | bytes 18436
  19.1 46.5 %copy-start.41 = (f32[1536]{0:T(1024)}, f32[1536]{0:T(1024)S(1)}, u32[]{:S(2)}) copy-start(f32[1536]{0:T(1024)S(1)} %get-tuple-element.414) | copy-start | bytes 18436
  34.3 8.8 copy-start.92
  34.3 8.8 copy-start.45
  34.3 8.9 copy-start.87
  51.6 19.3 %copy-start.23 = (f32[6,12,256]{2,1,0:T(8,128)}, f32[6,12,256]{2,1,0:T(8,128)S(1)}, u32[]{:S(2)}) copy-start(f32[6,12,256]{2,1,0:T(8,128)S(1)} %reduce_window_sum.39) | copy-start | bytes 221188
  51.8 19.1 %copy-start.17 = (f32[6,256,12]{1,0,2:T(8,128)}, f32[6,256,12]{1,0,2:T(8,128)S(1)}, u32[]{:S(2)}) copy-start(f32[6,256,12]{1,0,2:T(8,128)S(1)} %reshape.299) | copy-start | bytes 221188
  51.8 9.9 copy-start.31
  69.1 9.0 copy-start.10
  70.0 8.1 copy-start.49
  70.0 8.1 copy-start.58
  70.2 8.0 copy-start.80
  133.7 7.4 copy-start.36
  133.7 8.5 copy-start.24
  133.7 8.5 copy-start.30
  133.7 8.5 copy-start.51
  133.8 8.5 copy-start.91
  181.4 18.8 %copy-start.44 = (f32[768]{0:T(1024)S(1)}, f32[768]{0:T(1024)}, u32[]{:S(2)}) copy-start(f32[768]{0:T(1024)} %param.35) | copy-start | bytes 9220
  181.4 18.8 %copy-start.56 = (f32[1536]{0:T(1024)S(1)}, f32[1536]{0:T(1024)}, u32[]{:S(2)}) copy-start(f32[1536]{0:T(1024)} %get-tuple-element.412) | copy-start | bytes 18436
  243.1 19.8 %copy-start.4 = (f32[6,256,12,64]{1,0,3,2:T(8,128)S(1)}, f32[6,256,12,64]{1,0,3,2:T(8,128)}, u32[]{:S(2)}) copy-start(f32[6,256,12,64]{1,0,3,2:T(8,128)} %reshape.302) | copy-start | bytes 14155780
  321.8 18.7 %copy-start.7 = (f32[6,12,128,64]{3,2,1,0:T(8,128)S(1)}, f32[6,12,128,64]{3,2,1,0:T(8,128)}, u32[]{:S(2)}) copy-start(f32[6,12,128,64]{3,2,1,0:T(8,128)} %get-tuple-element.193) | copy-start | bytes 7077892
  321.8 18.7 %copy-start.12 = (bf16[1536,128]{1,0:T(8,128)(2,1)S(1)}, bf16[1536,128]{1,0:T(8,128)(2,1)}, u32[]{:S(2)}) copy-start(bf16[1536,128]{1,0:T(8,128)(2,1)} %copy-done.10) | copy-start | bytes 1179652
  321.8 27.5 %slice-start.12 = ((s8[4718592]{0:T(1024)(128)(4,1)}), s8[4194304]{0:T(1024)(128)(4,1)S(1)}, s32[]{:S(2)}) async-start(s8[4718592]{0:T(1024)(128)(4,1)} %bitcast.229), calls=%async_computation.14 | async-start | bytes 8388608
  340.5 8.8 slice-start.13
  340.5 8.8 copy-start.89
  340.6 15.6 %slice-start.2 = ((s8[6291456]{0:T(1024)(128)(4,1)}), s8[4194304]{0:T(1024)(128)(4,1)S(1)}, s32[]{:S(2)}) async-start(s8[6291456]{0:T(1024)(128)(4,1)} %bitcast.216), calls=%async_computation.4 | async-start | bytes 8388608
  356.2 23.7 %copy-start.14 = (f32[6,256,128]{2,1,0:T(8,128)S(1)}, f32[6,256,128]{2,1,0:T(8,128)}, u32[]{:S(2)}) copy-start(f32[6,256,128]{2,1,0:T(8,128)} %fusion.77) | copy-start | bytes 2359300
  356.2 25.5 %copy-start.9 = (bf16[1536,128]{1,0:T(8,128)(2,1)S(1)}, bf16[1536,128]{1,0:T(8,128)(2,1)}, u32[]{:S(2)}) copy-start(bf16[1536,128]{1,0:T(8,128)(2,1)} %get-tuple-element.400) | copy-start | bytes 1179652
  380.0 22.0 %copy-start.29 = (f32[6,256,12]{1,2,0:T(8,128)S(1)}, f32[6,256,12]{1,2,0:T(8,128)}, u32[]{:S(2)}) copy-start(f32[6,256,12]{1,2,0:T(8,128)} %copy-done.28) | copy-start | bytes 221188
  437.2 10.0 copy-start.38
  437.2 19.6 %slice-start = ((s8[4718592]{0:T(1024)(128)(4,1)}), s8[524288]{0:T(1024)(128)(4,1)S(1)}, s32[]{:S(2)}) async-start(s8[4718592]{0:T(1024)(128)(4,1)} %bitcast.205), calls=%async_computation.2 | async-start | bytes 1048576
  447.2 9.6 slice-start.1
  447.2 9.6 copy-start.40
  447.2 9.6 copy-start.42
  482.6 843.6 %all-reduce.32.cloned.1.call-start = ((), (), s32[]{:S(2)}) async-start(), calls=%async_computation | async-start | bytes 31653888 | tf_op jit(solution)/shard_map/psum | solution.py:164
  486.8 9.4 copy-start.21
  486.8 18.1 %slice-start.8 = ((s8[4718592]{0:T(1024)(128)(4,1)}), s8[4194304]{0:T(1024)(128)(4,1)S(1)}, s32[]{:S(2)}) async-start(s8[4718592]{0:T(1024)(128)(4,1)} %bitcast.223), calls=%async_computation.10 | async-start | bytes 8388608
  486.8 18.1 %slice-start.14 = ((s8[4718592]{0:T(1024)(128)(4,1)}), s8[4194304]{0:T(1024)(128)(4,1)S(1)}, s32[]{:S(2)}) async-start(s8[4718592]{0:T(1024)(128)(4,1)} %bitcast.231), calls=%async_computation.16 | async-start | bytes 8388608
  496.2 8.7 slice-start.9
  496.2 8.7 slice-start.15
  496.2 8.7 copy-start.57
  841.0 9.4 copy-start.85
  841.0 50.1 %copy-start.68 = (f32[1536]{0:T(1024)S(1)}, f32[1536]{0:T(1024)}, u32[]{:S(2)}) copy-start(f32[1536]{0:T(1024)} %get-tuple-element.408) | copy-start | bytes 18436
  1326.3 10.0 slice-start.16
  (66 other events, 261.8 us)
Sparse Core Ops, SparseCore 0:
  482.8 347.5 all-reduce.33
  840.2 486.0 all-reduce.31
where the time goes:
time: 1350 us
  waiting for transfers between devices  737 us (55%)
  matrix products  231 us (17%)
  local copies, waits for them, and re-layouts  161 us (12%)
  other arithmetic  145 us (11%)
  blocking collectives  55.2 us (4%)
  between operations  15.8 us (1%)
    psum x1, waiting for transfers between devices, body(): lax.psum((grad_norm, grad_gate, grad_input, grad_step, grad_state, grad_c...  418 us
    psum x1, waiting for transfers between devices, body(): mix = lax.psum(partial_mix, 'tensor')  319 us
    dot_general x3, matrix products, ssd_scan(): y_diag = jnp.einsum('chij,cjhp->cihp', mixing, x_blk, precision=HIGH)  66.6 us
    reshape x6, local copies, waits for them, and re-layouts, ssd_scan(): x_blk = values.reshape(blocks, group, heads, width)  54.7 us
    psum x1, blocking collectives, body(): lax.psum((grad_norm, grad_gate, grad_input, grad_step, grad_state, grad_c...  40.7 us
    dot_general x5, matrix products, back_dot(): lax.dot_general(left, right, (((1,), (1,)), ((), ())), preferred_element_...  36.6 us
    dot_general x3, matrix products, ssd_scan(): local_state = jnp.einsum('cjn,cjhp->chnp', b_blk, weighted, precision=HIGH)  31.2 us
    dot_general x5, matrix products, cross_dot(): lax.dot_general(left, right, (((0,), (0,)), ((), ())), preferred_element_...  31.2 us
  transfers between devices with their start and end apart: 2, of which 2 were waited for; matrix products, arithmetic and copies ran while one was open for 4% of the time, Pallas kernels for 0%

commit v1 on v0

--- a/solution.py
+++ b/solution.py
@@ -124,7 +124,8 @@
     gate_inverse = lax.rsqrt(square_sum / INNER + EPS)[:, None]
     gnormed = (gated * gate_inverse * gate_norm_gain[None, :]).astype(jnp.bfloat16)
     partial_mix = jnp.dot(gnormed, out_weight, preferred_element_type=jnp.float32)
-    mix = lax.psum(partial_mix, "tensor")
+    parts = lax.all_gather(partial_mix, "tensor", axis=0, tiled=False)
+    mix = parts.sum(axis=0)
     block_out = (hidden_f + valid * mix).astype(jnp.bfloat16)
     dmix = (cotangent.astype(jnp.float32) * valid).astype(jnp.bfloat16)
     grad_out = cross_dot(gnormed, dmix)

time: 1350 us -> 1420 us (1.052)
  waiting for transfers between devices: 737 us -> 780 us
  other arithmetic: 145 us -> 164 us
    all_gather x0 -> x1, waiting for transfers between devices: none -> 164 us  [body(): parts = lax.all_gather(partial_mix, 'tensor', axis=0, tiled=False)]
    psum x1, waiting for transfers between devices: 319 us -> 160 us  [body(): summed_back, states_full = lax.psum((local_back, d_states), 'tensor')]
    psum x1, waiting for transfers between devices: 418 us -> 455 us  [body(): lax.psum((grad_norm, grad_gate, grad_input, grad_step, grad_state, grad_c...]
    reduce_sum x0 -> x1, other arithmetic: none -> 19.6 us  [body(): mix = parts.sum(axis=0)]
  transfers between devices with their start and end apart: 2 -> 3, of which waited for: 2 -> 3; matrix products, arithmetic and copies ran while one was open for 4% -> 7% of each run, Pallas kernels for 0% -> 0%
where the time goes in v1:
time: 1420 us; the launch traced here: 1410 us
  waiting for transfers between devices  780 us (55%)
  matrix products  236 us (17%)
  other arithmetic  164 us (12%)
  local copies, waits for them, and re-layouts  161 us (11%)
  blocking collectives  53.4 us (4%)
  between operations  15.6 us (1%)
    psum x1, waiting for transfers between devices, body(): lax.psum((grad_norm, grad_gate, grad_input, grad_step, grad_state, grad_c...  455 us
    all_gather x1, waiting for transfers between devices, body(): parts = lax.all_gather(partial_mix, 'tensor', axis=0, tiled=False)  164 us
    psum x1, waiting for transfers between devices, body(): summed_back, states_full = lax.psum((local_back, d_states), 'tensor')  160 us
    dot_general x3, matrix products, ssd_scan(): y_diag = jnp.einsum('chij,cjhp->cihp', mixing, x_blk, precision=HIGH)  66.8 us
    reshape x6, local copies, waits for them, and re-layouts, ssd_scan(): x_blk = values.reshape(blocks, group, heads, width)  54.6 us
    dot_general x5, matrix products, back_dot(): lax.dot_general(left, right, (((1,), (1,)), ((), ())), preferred_element_...  42.5 us
    psum x1, blocking collectives, body(): lax.psum((grad_norm, grad_gate, grad_input, grad_step, grad_state, grad_c...  38.7 us
    dot_general x3, matrix products, ssd_scan(): local_state = jnp.einsum('cjn,cjhp->chnp', b_blk, weighted, precision=HIGH)  31.2 us
  transfers between devices with their start and end apart: 3, of which 3 were waited for; matrix products, arithmetic and copies ran while one was open for 7% of the time, Pallas kernels for 0%

profile of v1, /device:TPU:0, one launch (start us, length us, event | category | flops | bytes accessed | tf_op | source)
XLA Modules:
  0.0 1410.6 jit_solution(17556672709392373257)
XLA Ops:
  14.4 4.0 fusion.117
  19.1 6.4 multiply_convert_fusion.2
  25.5 8.5 reshape.328
  34.0 8.2 reshape.327
  42.9 4.3 compare_select_fusion.2
  51.4 9.9 copy.178
  77.8 42.6 %while.34 = (s32[]{:T(128)}, f32[12,128,64]{2,1,0:T(8,128)}, f32[6,12,128,64]{3,2,1,0:T(8,128)}, f32[6,12,1,1]{1,3,2,0:T(1,128)}, f32[6,12,128,64]{2,3,1,0:T(8,128)}, /*index=5*/f32[6,12]{1,0:T(8,128)}, s32[]{:T(128)}, s32[]{:T(128)}) while((s32[]{:T(128)}, f32[12,128,64]{2,1,0:T(8,128)}, f32[6,12,128,64]{3,2,1,0:T(8,128)}, ...), condition=%wide.region_4.5_spmd.clone, body=%wide.region_3.4_spmd.clone.sunk | while | flops 393219 | bytes 4327672 | solution.py:58
  120.4 5.4 copy.180
  125.9 5.9 fusion.120
  133.3 7.4 copy.176
  141.8 18.5 %fusion.40 = f32[6,256,12,64]{1,3,2,0:T(8,128)} fusion(f32[6,256,12,64]{1,3,2,0:T(8,128)} %copy.178, f32[6,256,12,64]{1,3,2,0:T(8,128)} %bitcast.229, f32[12]{0:T(128)S(1)} %copy-done.90, f32[6,256,12]{1,2,0:T(8,128)S(1)} %copy-done.30, bf16[6,256,12,64]{1,3,2,0:T(8,128)(2,1)} %copy.176, f32[6,12,256]{2,1,0:T(8,128)S(1)} %bitcast.260, ...), kind=kOutput, calls=%fused_computation.68 | convolution fusion | flops 3652190208 | bytes 18702384 | tf_op jit(solution)/shard_map/jvp(chij,cjhp->cihp)/dot_general | solution.py:45
  160.3 10.7 copy.219
  171.0 9.9 reshape.329
  181.0 10.3 multiply_reduce_fusion.11
  191.2 8.5 psum.126
  199.8 11.6 multiply_reduce_fusion.2
  211.3 6.2 psum.127
  217.6 12.3 multiply_reduce_fusion.3
  229.9 6.1 copy.185
  235.9 6.9 reshape.302
  242.8 19.6 %fusion.77 = f32[6,256,128]{2,1,0:T(8,128)} fusion(f32[6,12,128,64]{3,2,1,0:T(8,128)} %get-tuple-element.546, f32[6,256,12]{1,2,0:T(8,128)S(1)} %copy-done.30, f32[6,256,12,64]{1,0,3,2:T(8,128)} %reshape.302), kind=kOutput, calls=%fused_computation.129 | convolution fusion | flops 1813118976 | bytes 7938048 | tf_op jit(solution)/shard_map/transpose(jvp(cin,chnp->cihp))/dot_general | solution.py:60
  262.4 5.1 multiply_reduce_fusion.8
  267.5 4.9 fusion.70
  275.7 45.6 %while.35 = (s32[]{:T(128)}, f32[12,128,64]{2,1,0:T(8,128)}, f32[6,12,128,64]{3,2,1,0:T(8,128)}, f32[6,12]{1,0:T(8,128)}, f32[6,12,128,64]{2,3,1,0:T(8,128)}, /*...) while((s32[]{:T(128)}, f32[12,128,64]{2,1,0:T(8,128)}, ...), condition=%wide.region_12.13_spmd.clone, body=%wide.region_10.12_spmd.clone.sunk | while | flops 589816 | bytes 4719024 | solution.py:58
  321.3 18.7 %fusion.80 = f32[6,256,128]{2,1,0:T(8,128)S(1)} fusion(f32[6,12,128,64]{3,2,1,0:T(8,128)} %get-tuple-element.193, f32[6,256,12,64]{1,3,2,0:T(8,128)} %copy.178, f32[6,256,12]{1,2,0:T(8,128)} %copy-done.28), kind=kOutput, calls=%fused_computation.130 | convolution fusion | flops 1813118976 | bytes 7938048 | tf_op jit(solution)/shard_map/transpose(jvp(cjn,cjhp->chnp))/dot_general | solution.py:49
  340.1 8.7 multiply_reduce_fusion.9
  348.9 24.1 %fusion.11 = (f32[6,12,256]{2,1,0:T(8,128)}, f32[6,12,256]{2,1,0:T(8,128)}, f32[6,12,256]{2,1,0:T(8,128)}, f32[6,256,256]{2,1,0:T(8,128)S(1)}) fusion(f32[6,12,256]{2,1,0:T(8,128)S(1)} %bitcast.261, f32[6,256,256]{2,1,0:T(8,128)S(1)} %copy-done.26, f32[6,12,256]{2,1,0:T(8,128)S(1)} %copy-done.25, pred[6,256,256]{2,1,0:T(8,128)(4,1)S(1)} %copy-done.35, ...), kind=kOutput, calls=%fused_computation.31 | convolution fusion | flops 3694209024 | bytes 10985472 | tf_op jit(solution)/shard_map/transpose(jvp(chij,cjhp->cihp))/dot_general | solution.py:45
  379.6 14.9 %reduce-window.16 = f32[6,12,2,128]{3,1,2,0:T(8,128)S(1)} reduce-window(f32[6,12,2,128]{3,1,2,0:T(8,128)S(1)} %copy.201, f32[]{:T(128)} %constant.111.clone.1), window={size=1x1x1x128 pad=0_0x0_0x0_0x0_127}, to_apply=%region_19.20 | reduce-window | flops 2340864 | bytes 147460 | tf_op jit(solution)/shard_map/reduce-window.2
  395.1 24.2 %bitcast_add_fusion.2 = f32[6,256,12,64]{1,3,2,0:T(8,128)} fusion(f32[6,256,12,64]{1,3,2,0:T(8,128)} %get-tuple-element.427, f32[12]{0:T(128)} %param.34, f32[6,256,12]{1,2,0:T(8,128)S(1)} %copy-done.29, f32[6,12,256]{2,1,0:T(8,128)} %bitcast.259, f32[6,256,256]{2,1,0:T(8,128)} %fusion.119, f32[6,12,256]{2,1,0:T(8,128)S(1)} %copy-done.25, ...), kind=kOutput, calls=%fused_computation.62 | convolution fusion | flops 3652190208 | bytes 21061680 | tf_op jit(solution)/shard_map/transpose(jvp(chij,cjhp->cihp))/dot_general | solution.py:45
  419.3 10.7 copy.221
  430.1 10.0 reshape.330
  440.1 9.9 multiply_reduce_fusion.7
  458.4 6.5 fusion.122
  465.0 4.0 fusion.121
  470.5 5.2 convolution_add_fusion.1
  475.8 10.5 fusion.106
  486.6 3.9 fusion.97
  490.5 8.6 fusion.124
  499.1 5.6 fusion.123
  504.8 6.5 fusion.63
  511.2 160.3 %all-reduce.34.cloned.1.call-done = (f32[1536,1536]{1,0:T(8,128)}, f32[1536,256]{1,0:T(8,128)}) async-done(((f32[1536,1536]{1,0:T(8,128)}, f32[1536,256]{1,0:T(8,128)}), (f32[1536,1536]{1,0:T(8,128)}, f32[1536,256]{1,0:T(8,128)})) %all-reduce.34.cloned.1.call-update) | async-done | bytes 11010064 | tf_op jit(solution)/shard_map/psum | solution.py:150
  682.1 15.2 %fusion.21 = (f32[1536]{0:T(1024)S(1)}, f32[1536]{0:T(1024)S(1)}, f32[1536,1536]{1,0:T(8,128)}) fusion(bf16[1536,1536]{1,0:T(8,128)(2,1)} %param.21, f32[1536]{0:T(1024)S(1)} %copy-done.48, f32[1536]{0:T(1024)S(1)} %copy-done.55, f32[1536,1536]{1,0:T(8,128)} %get-tuple-element.361, bf16[1536,256]{1,0:T(8,128)(2,1)S(1)} %get-tuple-element.395, ...), kind=kOutput, calls=%fused_computation.43 | convolution fusion | flops 1226830848 | bytes 25190400 | tf_op jit(solution)/shard_map/dot_general | solution.py:72
  697.4 38.7 %all-reduce.26 = (f32[1536]{0:T(1024)}, f32[4,768]{1,0:T(4,128)}, f32[4,256]{1,0:T(4,128)}, f32[768]{0:T(1024)}, f32[256]{0:T(256)}, /*index=5*/f32[12]{0:T(128)}, f32[12]{0:T(128)}, f32[12]{0:T(128)}, f32[768]{0:T(1024)}) all-reduce(f32[1536]{0:T(1024)S(1)} %get-tuple-element.309, ...), channel_id=1, replica_groups=mesh['dp'=8,'tensor'=4] {'dp'}, use_global_device_ids=true, to_apply=%region_26.27 | all-reduce | flops 7460 | bytes 59680 | tf_op jit(solution)/shard_map/psum | solution.py:165
  736.1 164.4 %all-gather.3.cloned.1.call-done = f32[6144,1536]{1,0:T(8,128)} async-done(((f32[1536,1536]{1,0:T(8,128)}), f32[6144,1536]{1,0:T(8,128)}) %all-gather.3.cloned.1.call-update) | async-done | bytes 37748752 | tf_op jit(solution)/shard_map/all_gather | solution.py:127
  900.5 19.6 %reduce_sum.274 = f32[1536,1536]{1,0:T(8,128)} reduce(f32[4,1536,1536]{2,1,0:T(8,128)} %bitcast.226, f32[]{:T(128)} %constant.111.clone.1), dimensions={0}, to_apply=%region_7.8 | reduce | flops 7077888 | bytes 47185924 | tf_op jit(solution)/shard_map/reduce_sum | solution.py:128
  920.1 16.3 %fusion.13 = (f32[1536,1536]{1,0:T(8,128)}, bf16[1536,1536]{1,0:T(8,128)(2,1)}) fusion(bf16[1536,1536]{1,0:T(8,128)(2,1)} %param.37, bf16[1536,1536]{1,0:T(8,128)(2,1)} %param.21, f32[1536,1536]{1,0:T(8,128)} %get-tuple-element.428, f32[1536]{0:T(1024)S(1)} %broadcast_multiply_fusion.8, f32[1536]{0:T(1024)S(1)} %copy-done.68, f32[1536]{0:T(1024)S(1)} %copy-done.55, ...), kind=kLoop, calls=%fused_computation.35 | loop fusion | flops 25952256 | bytes 42498048 | tf_op jit(solution)/shard_map/sub | solution.py:157
  936.4 455.0 %all-reduce.32.cloned.1.call-done = (f32[1536,768]{1,0:T(8,128)}, f32[1536,768]{1,0:T(8,128)}, f32[1536,12]{0,1:T(8,128)}, f32[1536,256]{1,0:T(8,128)}, f32[768,1536]{1,0:T(8,128)}) async-done(((f32[1536,768]{1,0:T(8,128)}, f32[1536,768]{1,0:T(8,128)}, f32[1536,12]{0,1:T(8,128)}, f32[1536,256]{1,0:T(8,128)}, f32[768,1536]{1,0:T(8,128)}), (f32[1536,768]{1,0:T(8,128)}, f32[1536,768]{1,0:T(8,128)}, ...) | async-done | bytes 15802384 | tf_op jit(solution)/shard_map/psum | solution.py:165
  1391.4 5.2 copy.308
  (402 shorter events, 157.7 us)
Async XLA Ops:
  7.2 173.8 %copy-start = (bf16[1536,768]{1,0:T(8,128)(2,1)S(1)}, bf16[1536,768]{1,0:T(8,128)(2,1)}, u32[]{:S(2)}) copy-start(bf16[1536,768]{1,0:T(8,128)(2,1)} %param.24) | copy-start | bytes 7077892
  7.2 664.3 %all-reduce.34.cloned.1.call-start = ((), (), s32[]{:S(2)}) async-start(), calls=%async_computation.2 | async-start | bytes 22020096 | tf_op jit(solution)/shard_map/psum | solution.py:150
  19.0 46.1 %copy-start.37 = (f32[1536]{0:T(1024)}, f32[1536]{0:T(1024)S(1)}, u32[]{:S(2)}) copy-start(f32[1536]{0:T(1024)S(1)} %get-tuple-element.414) | copy-start | bytes 18436
  19.0 46.1 %copy-start.39 = (f32[1536]{0:T(1024)}, f32[1536]{0:T(1024)S(1)}, u32[]{:S(2)}) copy-start(f32[1536]{0:T(1024)S(1)} %get-tuple-element.412) | copy-start | bytes 18436
  19.0 46.2 %copy-start.41 = (f32[1536]{0:T(1024)}, f32[1536]{0:T(1024)S(1)}, u32[]{:S(2)}) copy-start(f32[1536]{0:T(1024)S(1)} %get-tuple-element.413) | copy-start | bytes 18436
  34.0 8.8 copy-start.91
  34.0 8.8 copy-start.45
  34.0 8.8 copy-start.87
  51.2 19.3 %copy-start.23 = (f32[6,12,256]{2,1,0:T(8,128)}, f32[6,12,256]{2,1,0:T(8,128)S(1)}, u32[]{:S(2)}) copy-start(f32[6,12,256]{2,1,0:T(8,128)S(1)} %reduce_window_sum.39) | copy-start | bytes 221188
  51.4 19.1 %copy-start.17 = (f32[6,256,12]{1,0,2:T(8,128)}, f32[6,256,12]{1,0,2:T(8,128)S(1)}, u32[]{:S(2)}) copy-start(f32[6,256,12]{1,0,2:T(8,128)S(1)} %reshape.299) | copy-start | bytes 221188
  51.4 9.9 copy-start.31
  68.8 9.0 copy-start.10
  69.7 8.1 copy-start.49
  69.7 8.1 copy-start.58
  133.3 8.5 copy-start.24
  133.3 8.5 copy-start.30
  133.3 8.5 copy-start.51
  133.3 8.5 copy-start.90
  181.0 18.8 %copy-start.44 = (f32[768]{0:T(1024)S(1)}, f32[768]{0:T(1024)}, u32[]{:S(2)}) copy-start(f32[768]{0:T(1024)} %param.35) | copy-start | bytes 9220
  181.0 18.8 %copy-start.56 = (f32[1536]{0:T(1024)S(1)}, f32[1536]{0:T(1024)}, u32[]{:S(2)}) copy-start(f32[1536]{0:T(1024)} %get-tuple-element.411) | copy-start | bytes 18436
  242.8 19.6 %copy-start.4 = (f32[6,256,12,64]{1,0,3,2:T(8,128)S(1)}, f32[6,256,12,64]{1,0,3,2:T(8,128)}, u32[]{:S(2)}) copy-start(f32[6,256,12,64]{1,0,3,2:T(8,128)} %reshape.302) | copy-start | bytes 14155780
  321.3 18.7 %copy-start.7 = (f32[6,12,128,64]{3,2,1,0:T(8,128)S(1)}, f32[6,12,128,64]{3,2,1,0:T(8,128)}, u32[]{:S(2)}) copy-start(f32[6,12,128,64]{3,2,1,0:T(8,128)} %get-tuple-element.193) | copy-start | bytes 7077892
  321.3 18.7 %copy-start.12 = (bf16[1536,128]{1,0:T(8,128)(2,1)S(1)}, bf16[1536,128]{1,0:T(8,128)(2,1)}, u32[]{:S(2)}) copy-start(bf16[1536,128]{1,0:T(8,128)(2,1)} %copy-done.10) | copy-start | bytes 1179652
  321.3 27.5 %slice-start.2 = ((s8[6291456]{0:T(1024)(128)(4,1)}), s8[4194304]{0:T(1024)(128)(4,1)S(1)}, s32[]{:S(2)}) async-start(s8[6291456]{0:T(1024)(128)(4,1)} %bitcast.217), calls=%async_computation.5 | async-start | bytes 8388608
  340.0 8.8 slice-start.3
  340.0 8.8 copy-start.22
  340.0 8.8 copy-start.25
  340.0 8.8 copy-start.26
  340.0 8.8 copy-start.35
  340.1 8.8 copy-start.52
  348.9 24.2 %copy-start.14 = (f32[6,256,128]{2,1,0:T(8,128)S(1)}, f32[6,256,128]{2,1,0:T(8,128)}, u32[]{:S(2)}) copy-start(f32[6,256,128]{2,1,0:T(8,128)} %fusion.77) | copy-start | bytes 2359300
  348.9 26.0 %copy-start.9 = (bf16[1536,128]{1,0:T(8,128)(2,1)S(1)}, bf16[1536,128]{1,0:T(8,128)(2,1)}, u32[]{:S(2)}) copy-start(bf16[1536,128]{1,0:T(8,128)(2,1)} %get-tuple-element.399) | copy-start | bytes 1179652
  373.1 22.0 %copy-start.29 = (f32[6,256,12]{1,2,0:T(8,128)S(1)}, f32[6,256,12]{1,2,0:T(8,128)}, u32[]{:S(2)}) copy-start(f32[6,256,12]{1,2,0:T(8,128)} %copy-done.28) | copy-start | bytes 221188
  430.1 10.0 copy-start.38
  430.1 19.9 %slice-start = ((s8[4718592]{0:T(1024)(128)(4,1)}), s8[524288]{0:T(1024)(128)(4,1)S(1)}, s32[]{:S(2)}) async-start(s8[4718592]{0:T(1024)(128)(4,1)} %bitcast.206), calls=%async_computation.3 | async-start | bytes 1048576
  440.1 9.9 slice-start.1
  440.1 9.9 copy-start.40
  440.1 9.9 copy-start.42
  475.7 424.8 %all-gather.3.cloned.1.call-start = ((), (), s32[]{:S(2)}) async-start(), calls=%async_computation | async-start | bytes 47185920 | tf_op jit(solution)/shard_map/all_gather | solution.py:127
  486.3 12.8 slice-start.6
  486.3 905.0 %all-reduce.32.cloned.1.call-start = ((), (), s32[]{:S(2)}) async-start(), calls=%async_computation.1 | async-start | bytes 31653888 | tf_op jit(solution)/shard_map/psum | solution.py:165
  490.5 8.6 slice-start.7
  490.5 8.6 copy-start.21
  490.5 14.3 %slice-start.10 = ((s8[4718592]{0:T(1024)(128)(4,1)}), s8[4194304]{0:T(1024)(128)(4,1)S(1)}, s32[]{:S(2)}) async-start(s8[4718592]{0:T(1024)(128)(4,1)} %bitcast.227), calls=%async_computation.13 | async-start | bytes 8388608
  490.5 14.3 %slice-start.14 = ((s8[4718592]{0:T(1024)(128)(4,1)}), s8[4194304]{0:T(1024)(128)(4,1)S(1)}, s32[]{:S(2)}) async-start(s8[4718592]{0:T(1024)(128)(4,1)} %bitcast.233), calls=%async_computation.17 | async-start | bytes 8388608
  682.1 15.3 %copy-start.85 = (f32[768]{0:T(1024)S(1)}, f32[768]{0:T(1024)}, u32[]{:S(2)}) copy-start(f32[768]{0:T(1024)} %get-tuple-element.311) | copy-start | bytes 9220
  900.5 19.6 %copy-start.68 = (f32[1536]{0:T(1024)S(1)}, f32[1536]{0:T(1024)}, u32[]{:S(2)}) copy-start(f32[1536]{0:T(1024)} %get-tuple-element.407) | copy-start | bytes 18436
  1391.4 10.0 slice-start.16
  (66 other events, 260.5 us)
Sparse Core Ops, SparseCore 0:
  475.8 195.6 all-reduce.33
  673.1 227.3 all-gather.2
  906.8 484.5 all-reduce.31
